TPU v7x, 32 devices: a whole 2x2x4 slice. The times are simulated.
32 devices in a mesh: dp: 4 (over y, x), ctx: 4 (over z), tensor: 2 (over core).
Axes of the slice: x: 2, y: 2, z: 4, core: 2. Of those that a mesh axis runs over, the one named last changes fastest.
Arguments:
- hidden: bfloat16 [4, 1024, 1024], P('dp', 'ctx'), may hold values from -6 to 6
- segment_ids: int32 [4, 1024], P('dp', 'ctx'), may hold values from 0 to 5, as said below
- cotangent: bfloat16 [4, 1024, 1024], P('dp', 'ctx'), may hold values from -6 to 6
- input_gain: float32 [1024], replicated, may hold values from 0.5 to 1.5
- gate_weight: bfloat16 [1024, 2048], P('dp', 'tensor'), may hold values from -0.1875 to 0.1875
- value_weight: bfloat16 [1024, 2048], P('dp', 'tensor'), may hold values from -0.1875 to 0.1875
- state_weight: bfloat16 [1024, 256], P('dp'), may hold values from -0.1875 to 0.1875
- step_weight: bfloat16 [1024, 32], P('dp', 'tensor'), may hold values from -0.1875 to 0.1875
- conv_weight: float32 [4, 2304], replicated, may hold values from -3 to 3
- conv_bias: float32 [2304], replicated, may hold values from -3 to 3
- step_bias: float32 [32], replicated, may hold values from -4 to -1
- decay_log: float32 [32], replicated, may hold values from -6.5 to -1.5
- skip_gain: float32 [32], replicated, may hold values from 0.5 to 1.5
- mixer_gain: float32 [2048], replicated, may hold values from 0.5 to 1.5
- out_weight: bfloat16 [2048, 1024], P('tensor', 'dp'), may hold values from -0.125 to 0.125
Outputs:
- output: bfloat16 [4, 1024, 1024], P('dp', 'ctx')
- grad_hidden: float32 [4, 1024, 1024], P('dp', 'ctx')
- grad_input_gain: float32 [1024], replicated
- grad_gate_weight: float32 [1024, 2048], P('dp', 'tensor')
- grad_value_weight: float32 [1024, 2048], P('dp', 'tensor')
- grad_state_weight: float32 [1024, 256], P('dp')
- grad_step_weight: float32 [1024, 32], P('dp', 'tensor')
- grad_conv_weight: float32 [4, 2304], replicated
- grad_conv_bias: float32 [2304], replicated
- grad_step_bias: float32 [32], replicated
- grad_decay_log: float32 [32], replicated
- grad_skip_gain: float32 [32], replicated
- grad_mixer_gain: float32 [2048], replicated
- grad_out_weight: float32 [2048, 1024], P('tensor', 'dp')
Inputs may be any that keep to these rules, and one draw needn't show every extreme that they name: `segment_ids`: within each sequence the ids start at 0, never fall and rise by one at each new document. Every document has 200 to 512 tokens, except the last one of a sequence, which may be cut short by the sequence's end. The first document of the first sequence has exactly 512 tokens; every document of the last sequence has exactly 200 tokens (the final one possibly cut short).
All inputs are finite; a program needn't handle non-finite values.
Results may differ from a plain program's by a relative error of at most 0.014.
Values may be sent and summed in bfloat16 or wider, within the bound.
A program may use at most 192 MiB of HBM per device.

v0:
```python
from functools import partial

import jax
import jax.numpy as jnp
from jax import lax
from jax.sharding import PartitionSpec as P

GROUP = 128


epsilon = 1e-05
highest = lax.Precision.HIGHEST


def shifted(array, axis, by):
    size = lax.axis_size(axis)
    pairs = [(i, i + by) for i in range(size) if 0 <= i + by < size]
    return lax.ppermute(array, axis, pairs)


def carried_in_2(array, axis, combine, identity):
    size, here = (lax.axis_size(axis), lax.axis_index(axis))
    everything = jax.tree.map(
        lambda part, kind: lax.all_gather(part.astype(kind), axis),
        array,
        (jnp.bfloat16, jnp.bfloat16),
    )
    start = jax.tree.map(
        lambda part, zero: jnp.broadcast_to(jnp.asarray(zero, part.dtype), part.shape),
        array,
        identity,
    )

    def turn(k, before):
        reached = k < here
        new = combine(
            before, jax.tree.map(lambda part, own: part[k].astype(own.dtype), everything, array)
        )
        return jax.tree.map(lambda a, b: jnp.where(reached, a, b), new, before)

    return lax.fori_loop(0, size, turn, start)


def prefix(array, axis, join, neutral):
    count = lax.axis_size(axis)
    place = lax.axis_index(axis)
    ahead = count - 1 - place
    gathered = jax.tree.map(
        lambda a, kind: lax.all_gather(a.astype(kind), axis),
        array,
        jax.tree.map(lambda a: jnp.bfloat16 if a.dtype == jnp.float32 else a.dtype, array),
    )
    state = jax.tree.map(lambda a, e: jnp.zeros_like(a) + jnp.asarray(e, a.dtype), array, neutral)

    def one(turn, state):
        source = count - 1 - turn
        return join(
            state,
            jax.tree.map(
                lambda a, own: lax.dynamic_index_in_dim(a, source, 0, False).astype(own.dtype),
                gathered,
                array,
            ),
        )

    return lax.fori_loop(0, ahead, one, state)


def rms_scale(values, scaling):
    return values * lax.rsqrt(jnp.mean(values * values, axis=-1, keepdims=True) + epsilon) * scaling


def group_step(carry, item, rates):
    values, inputs_b, inputs_c, delta, segments, previous = item
    log_decay = delta * rates[None, :]
    running = jnp.cumsum(log_decay, axis=0)
    length = segments.shape[0]
    order = jnp.arange(length)
    allowed = (segments[:, None] == segments[None, :]) & (order[:, None] >= order[None, :])
    spread = running.T[:, :, None] - running.T[:, None, :]
    decay = jnp.where(allowed[None], jnp.exp(jnp.where(allowed[None], spread, 0.0)), 0.0)
    scores = jnp.dot(inputs_c, inputs_b.T, precision=highest)
    mixing = decay * scores[None] * delta.T[:, None, :]
    inner = jnp.einsum("hts,shp->thp", mixing, values, precision=highest)
    entry = jnp.exp(running) * (segments == previous).astype(jnp.float32)[:, None]
    carried = jnp.einsum("tn,hpn->thp", inputs_c, carry, precision=highest) * entry[:, :, None]
    tail = (
        jnp.exp(running[-1][None, :] - running)
        * (segments == segments[-1]).astype(jnp.float32)[:, None]
        * delta
    )
    fade = jnp.exp(running[-1]) * (segments[-1] == previous).astype(jnp.float32)
    update = jnp.einsum("sh,shp,sn->hpn", tail, values, inputs_b, precision=highest)
    return (carry * fade[:, None, None] + update, inner + carried)


def combine_states(earlier, later):
    return (earlier[0] * later[0], later[0][:, None, None] * earlier[1] + later[1])


def body(
    hidden,
    segment_ids,
    cotangent,
    input_gain,
    gate_weight,
    value_weight,
    state_weight,
    step_weight,
    conv_weight,
    conv_bias,
    step_bias,
    decay_log,
    skip_gain,
    mixer_gain,
    out_weight,
):
    tokens = hidden[0]
    wrapped = segment_ids[0] % 128
    cotangent_rows = cotangent[0]
    length = tokens.shape[0]
    width = tokens.shape[1]
    shard = lax.axis_index("tensor")
    shards = lax.axis_size("tensor")
    full_gate, full_value, full_state, full_step, full_out = (
        lax.all_gather(gate_weight, "dp", axis=0, tiled=True),
        lax.all_gather(value_weight, "dp", axis=0, tiled=True),
        lax.all_gather(state_weight, "dp", axis=0, tiled=True),
        lax.all_gather(step_weight, "dp", axis=0, tiled=True),
        lax.all_gather(out_weight, "dp", axis=1, tiled=True),
    )
    local_width = full_gate.shape[1]
    local_heads = full_step.shape[1]
    head_size = local_width // local_heads
    inner_width = local_width * shards
    states = full_state.shape[1] // 2
    reach = conv_weight.shape[0] - 1
    base = tokens.astype(jnp.float32)
    normed_full, norm_back = jax.vjp(rms_scale, base, input_gain)
    normed = normed_full.astype(jnp.bfloat16)
    gate = jnp.dot(normed, full_gate, preferred_element_type=jnp.float32)
    value_pre = jnp.dot(normed, full_value, preferred_element_type=jnp.float32).astype(jnp.bfloat16)
    state_pre = jnp.dot(normed, full_state, preferred_element_type=jnp.float32).astype(jnp.bfloat16)
    raw_step = jnp.dot(normed, full_step, preferred_element_type=jnp.float32)
    conv_input = jnp.concatenate([value_pre, state_pre], 1)
    edge_rows, edge_ids = shifted(
        (conv_input[length - reach :], wrapped[length - reach :].astype(jnp.bfloat16)), "ctx", 1
    )
    padded = jnp.concatenate([edge_rows, conv_input], 0).astype(jnp.float32)
    padded_ids = jnp.concatenate([edge_ids.astype(jnp.int32), wrapped])
    before = padded_ids[reach - 1]
    kernel = jnp.concatenate(
        [
            lax.dynamic_slice_in_dim(conv_weight, shard * local_width, local_width, 1),
            conv_weight[:, inner_width:],
        ],
        1,
    )
    offset = jnp.concatenate(
        [
            lax.dynamic_slice_in_dim(conv_bias, shard * local_width, local_width, 0),
            conv_bias[inner_width:],
        ],
        0,
    )
    local_bias = lax.dynamic_slice_in_dim(step_bias, shard * local_heads, local_heads, 0)
    local_decay = lax.dynamic_slice_in_dim(decay_log, shard * local_heads, local_heads, 0)
    local_skip = lax.dynamic_slice_in_dim(skip_gain, shard * local_heads, local_heads, 0)
    local_gain = lax.dynamic_slice_in_dim(mixer_gain, shard * local_width, local_width, 0)

    def activate(padded_rows, raw_rows, taps, shift_bias, bias_heads):
        total = jnp.broadcast_to(shift_bias[None, :], (length, shift_bias.shape[0]))
        for lag in range(reach + 1):
            begin = reach - lag
            same = (padded_ids[begin : begin + length] == wrapped).astype(jnp.float32)
            total = total + taps[lag][None, :] * padded_rows[begin : begin + length] * same[:, None]
        activated = jax.nn.silu(total)
        values = activated[:, :local_width].reshape(length, local_heads, head_size)
        return (
            values,
            activated[:, local_width : local_width + states],
            activated[:, local_width + states :],
            jax.nn.softplus(raw_rows + bias_heads[None, :]),
        )

    (values, inputs_b, inputs_c, delta), activate_back = jax.vjp(
        activate, padded, raw_step, kernel, offset, local_bias
    )

    def block(values_in, map_in, map_out, delta_in, decay_in, skip_in):
        rates = -jnp.exp(decay_in)
        count = length // GROUP
        previous = jnp.concatenate([before[None], wrapped[GROUP - 1 :: GROUP][: count - 1]])
        items = (
            values_in.reshape(count, GROUP, local_heads, head_size),
            map_in.reshape(count, GROUP, states),
            map_out.reshape(count, GROUP, states),
            delta_in.reshape(count, GROUP, local_heads),
            wrapped.reshape(count, GROUP),
            previous,
        )
        final, outputs = lax.scan(
            partial(group_step, rates=rates),
            jnp.zeros((local_heads, head_size, states), jnp.float32),
            items,
        )
        mixed = outputs.reshape(length, local_heads, head_size) + skip_in[None, :, None] * values_in
        through = jnp.exp(jnp.sum(delta_in * rates[None, :], axis=0)) * (
            wrapped[-1] == before
        ).astype(jnp.float32)
        return (mixed, through, final)

    (mixed_own, through, final), block_back = jax.vjp(
        block, values, inputs_b, inputs_c, delta, local_decay, local_skip
    )
    carried_in = carried_in_2(
        (through, final), "ctx", combine_states, (jnp.ones_like(through), jnp.zeros_like(final))
    )
    entering = carried_in[1]

    def enter(map_out, delta_in, decay_in, state_in):
        running = jnp.cumsum(delta_in * (-jnp.exp(decay_in))[None, :], axis=0)
        scaling = jnp.exp(running) * (wrapped == before).astype(jnp.float32)[:, None]
        return jnp.einsum("tn,hpn->thp", map_out, state_in, precision=highest) * scaling[:, :, None]

    added, enter_back = jax.vjp(enter, inputs_c, delta, local_decay, entering)
    mixed = (mixed_own + added).reshape(length, local_width)
    silu_gate = jax.nn.silu(gate)
    product = mixed * silu_gate
    squares = lax.psum(jnp.sum(product * product, axis=1), "tensor")
    scale = lax.rsqrt(squares / inner_width + epsilon)
    unit = product * scale[:, None]
    gated = (unit * local_gain[None, :]).astype(jnp.bfloat16)
    branch_out = jnp.dot(gated, full_out, preferred_element_type=jnp.float32)
    summed = lax.psum(branch_out.astype(jnp.bfloat16), "tensor").astype(jnp.float32)
    result = (base + summed).astype(jnp.bfloat16)
    grad_gated = jnp.dot(cotangent_rows, full_out.T, preferred_element_type=jnp.float32)
    grad_out = jnp.dot(gated.T, cotangent_rows, preferred_element_type=jnp.float32)
    grad_mgain = jnp.sum(grad_gated * unit, axis=0)
    grad_unit = grad_gated * local_gain[None, :]
    project = lax.psum(jnp.sum(grad_unit * unit, axis=1), "tensor")
    grad_product = scale[:, None] * (grad_unit - unit * (project / inner_width)[:, None])
    grad_mixed = (grad_product * silu_gate).reshape(length, local_heads, head_size)
    sigma = jax.nn.sigmoid(gate)
    grad_gate = grad_product * mixed * sigma * (1.0 + gate * (1.0 - sigma))
    map_one, delta_one, decay_one, grad_entering = enter_back(grad_mixed)
    carried_out = prefix(
        (through, grad_entering),
        "ctx",
        combine_states,
        (jnp.ones_like(through), jnp.zeros_like(grad_entering)),
    )
    grad_final = carried_out[1]
    grad_through = jnp.sum(grad_final * entering, axis=(1, 2))
    grad_values, grad_map_in, map_two, delta_two, decay_two, grad_skip = block_back(
        (grad_mixed, grad_through, grad_final)
    )
    grad_padded, grad_raw, grad_kernel, grad_offset, grad_bias = activate_back(
        (grad_values, grad_map_in, map_one + map_two, delta_one + delta_two)
    )
    edge_grad = shifted(grad_padded[:reach], "ctx", -1)
    grad_input = grad_padded[reach:].at[length - reach :].add(edge_grad)
    low_gate = grad_gate.astype(jnp.bfloat16)
    low_input = grad_input.astype(jnp.bfloat16)
    low_step = grad_raw.astype(jnp.bfloat16)
    normed_part = (
        jnp.dot(low_gate, full_gate.T, preferred_element_type=jnp.float32)
        + jnp.dot(low_input[:, :local_width], full_value.T, preferred_element_type=jnp.float32)
        + jnp.dot(low_input[:, local_width:], full_state.T, preferred_element_type=jnp.float32)
        + jnp.dot(low_step, full_step.T, preferred_element_type=jnp.float32)
    )
    grad_normed = lax.psum(normed_part.astype(jnp.bfloat16), "tensor").astype(jnp.float32)
    grad_base, grad_gain = norm_back(grad_normed)
    grad_tokens = cotangent_rows.astype(jnp.float32) + grad_base
    grad_gate_w = jnp.dot(normed.T, low_gate, preferred_element_type=jnp.float32)
    grad_value_w = jnp.dot(normed.T, low_input[:, :local_width], preferred_element_type=jnp.float32)
    grad_state_w = jnp.dot(normed.T, low_input[:, local_width:], preferred_element_type=jnp.float32)
    grad_step_w = jnp.dot(normed.T, low_step, preferred_element_type=jnp.float32)
    pieces = (
        lax.psum_scatter(
            grad_gate_w.astype(jnp.bfloat16), "dp", scatter_dimension=0, tiled=True
        ).astype(jnp.float32),
        lax.psum_scatter(
            grad_value_w.astype(jnp.bfloat16), "dp", scatter_dimension=0, tiled=True
        ).astype(jnp.float32),
        lax.psum_scatter(
            grad_step_w.astype(jnp.bfloat16), "dp", scatter_dimension=0, tiled=True
        ).astype(jnp.float32),
        lax.psum_scatter(
            grad_out.astype(jnp.bfloat16), "dp", scatter_dimension=1, tiled=True
        ).astype(jnp.float32),
    )
    sums = (
        lax.psum(pieces[0].astype(jnp.bfloat16), "ctx").astype(jnp.float32),
        lax.psum(pieces[1].astype(jnp.bfloat16), "ctx").astype(jnp.float32),
        lax.psum(pieces[2].astype(jnp.bfloat16), "ctx").astype(jnp.float32),
        lax.psum(pieces[3].astype(jnp.bfloat16), "ctx").astype(jnp.float32),
    )
    halves = width // shards
    keep_half = (jnp.arange(width) // halves == shard).astype(jnp.float32)
    gain_term = grad_gain * keep_half
    kernel_term = jnp.zeros((reach + 1, inner_width + 2 * states), jnp.float32)
    kernel_term = lax.dynamic_update_slice(
        kernel_term, grad_kernel[:, :local_width], (0, shard * local_width)
    )
    kernel_term = kernel_term.at[:, inner_width:].set(grad_kernel[:, local_width:])
    offset_term = jnp.zeros((inner_width + 2 * states,), jnp.float32)
    offset_term = lax.dynamic_update_slice(
        offset_term, grad_offset[:local_width], (shard * local_width,)
    )
    offset_term = offset_term.at[inner_width:].set(grad_offset[local_width:])
    heads_total = local_heads * shards
    bias_term = lax.dynamic_update_slice(
        jnp.zeros((heads_total,), jnp.float32), grad_bias, (shard * local_heads,)
    )
    decay_term = lax.dynamic_update_slice(
        jnp.zeros((heads_total,), jnp.float32), decay_one + decay_two, (shard * local_heads,)
    )
    skip_term = lax.dynamic_update_slice(
        jnp.zeros((heads_total,), jnp.float32), grad_skip, (shard * local_heads,)
    )
    mgain_term = lax.dynamic_update_slice(
        jnp.zeros((inner_width,), jnp.float32), grad_mgain, (shard * local_width,)
    )
    totals = lax.psum(
        (
            gain_term,
            kernel_term,
            offset_term,
            bias_term,
            decay_term,
            skip_term,
            mgain_term,
            grad_state_w,
        ),
        ("dp", "ctx", "tensor"),
    )
    rows = state_weight.shape[0]
    state_rows = lax.dynamic_slice_in_dim(totals[7], lax.axis_index("dp") * rows, rows, 0)
    return (
        result[None],
        grad_tokens[None],
        totals[0],
        sums[0],
        sums[1],
        state_rows,
        sums[2],
        totals[1],
        totals[2],
        totals[3],
        totals[4],
        totals[5],
        totals[6],
        sums[3],
    )


def solution(mesh):
    in_specs = (
        P("dp", "ctx", None),
        P("dp", "ctx"),
        P("dp", "ctx", None),
        P(),
        P("dp", "tensor"),
        P("dp", "tensor"),
        P("dp", None),
        P("dp", "tensor"),
        P(),
        P(),
        P(),
        P(),
        P(),
        P(),
        P("tensor", "dp"),
    )
    out_specs = (
        P("dp", "ctx", None),
        P("dp", "ctx", None),
        P(),
        P("dp", "tensor"),
        P("dp", "tensor"),
        P("dp", None),
        P("dp", "tensor"),
        P(),
        P(),
        P(),
        P(),
        P(),
        P(),
        P("tensor", "dp"),
    )
    return jax.shard_map(body, mesh=mesh, in_specs=in_specs, out_specs=out_specs, check_vma=False)
```

profile of v0, /device:TPU:0, one launch (start us, length us, event | category | flops | bytes accessed | tf_op | source)
XLA Modules:
  0.0 727.3 jit_solution(9285679522740016677)
XLA Ops:
  8.9 4.9 collective-permute-start
  15.5 8.6 %all_gather.33 = bf16[1024,16]{0,1:T(8,128)(2,1)S(1)} all-gather(bf16[256,16]{0,1:T(8,128)(2,1)} %param.36), channel_id=1, replica_groups=mesh['dp'=4,'ctx'=4,'tensor'=2] {'dp'}, dimensions={0}, use_global_device_ids=true | all-gather | bytes 40960 | tf_op jit(solution)/shard_map/all_gather | solution.py:129
  26.1 2.6 compare_select_fusion.3
  29.5 13.2 %all_gather.35 = bf16[1024,256]{1,0:T(8,128)(2,1)S(1)} all-gather(bf16[256,256]{1,0:T(8,128)(2,1)S(1)} %copy-done.49), channel_id=1, replica_groups=mesh['dp'=4,'ctx'=4,'tensor'=2] {'dp'}, dimensions={0}, use_global_device_ids=true | all-gather | bytes 655360 | tf_op jit(solution)/shard_map/all_gather | solution.py:128
  46.3 2.9 all-gather.9.cloned.1.call-done
  49.2 2.3 convolution_convert_fusion.4
  51.6 3.4 collective-permute-start.1
  56.6 2.1 fusion.109
  67.7 120.8 %while.117 = (s32[]{:T(128)}, f32[16,64,128]{2,1,0:T(8,128)S(1)}, f32[2,128,16,64]{1,0,3,2:T(2,128)}, pred[2,16,128,128]{3,2,1,0:T(32,128)(4,1)}, f32[2,16,128,1...) while((s32[]{:T(128)}, f32[16,64,128]{2,1,0:T(8,128)S(1)}, ...), condition=%wide.region_3.4_spmd.clone, body=%wide.region_1.3_spmd.clone.sunk | while | flops 633275392 | bytes 14210707 | solution.py:202
  68.9 1.8 constant_dynamic-update-slice_fusion.16
  76.4 3.3 multiply_dynamic-update-slice_fusion.3
  85.8 3.0 fusion.255
  88.8 13.1 %dynamic_update_slice.320 = f32[2,128,16,64]{1,0,3,2:T(2,128)} dynamic-update-slice(f32[2,128,16,64]{1,0,3,2:T(2,128)} %get-tuple-element.2790, f32[1,128,16,64]{1,0,3,2:T(1,128)} %bitcast.578, s32[]{:T(128)} %get-tuple-element.2788, s32[]{:T(128)} %constant.380.clone.1..sunk.1, s32[]{:T(128)} %constant.380.clone.1..sunk.1, s32[]{:T(128)} %constant.380.clone.1..sunk.1) | dynamic-update-slice | bytes 1048580 | tf_op jit(solution)/shard_map/jvp()/while/body/jit(dynamic_update_index_in_dim)/dynamic_update_slice | solution.py:202
  129.3 1.8 constant_dynamic-update-slice_fusion.16
  136.8 3.4 multiply_dynamic-update-slice_fusion.3
  146.2 3.0 fusion.255
  149.2 13.1 %dynamic_update_slice.320 = f32[2,128,16,64]{1,0,3,2:T(2,128)} dynamic-update-slice(f32[2,128,16,64]{1,0,3,2:T(2,128)} %get-tuple-element.2790, f32[1,128,16,64]{1,0,3,2:T(1,128)} %bitcast.578, s32[]{:T(128)} %get-tuple-element.2788, s32[]{:T(128)} %constant.380.clone.1..sunk.1, s32[]{:T(128)} %constant.380.clone.1..sunk.1, s32[]{:T(128)} %constant.380.clone.1..sunk.1) | dynamic-update-slice | bytes 1048580 | tf_op jit(solution)/shard_map/jvp()/while/body/jit(dynamic_update_index_in_dim)/dynamic_update_slice | solution.py:202
  195.1 13.2 %all-reduce.13 = bf16[64]{0:T(256)(128)(2,1)S(1)} all-reduce(bf16[64]{0:T(256)(128)(2,1)S(1)} %dynamic-update-slice.8), channel_id=2, replica_groups=mesh['dp'=4,'ctx'=4,'tensor'=2] {'ctx'}, use_global_device_ids=true, to_apply=%add.13 | all-reduce | flops 64 | bytes 256
  208.5 3.0 reshape.727
  211.5 6.9 all-gather.15.cloned.1.call-done
  218.4 4.6 while.118
  223.1 3.8 multiply_add_fusion.2
  226.9 2.7 copy.192
  229.5 25.4 %all-gather.11.cloned.1.call-done = bf16[1024,1024]{1,0:T(8,128)(2,1)} async-done(((bf16[256,1024]{1,0:T(8,128)(2,1)}), bf16[1024,1024]{1,0:T(8,128)(2,1)}) %all-gather.11.cloned.1.call-update) | async-done | bytes 2097168 | tf_op jit(solution)/shard_map/all_gather | solution.py:126
  254.9 3.7 multiply_reduce_fusion.9
  258.6 2.4 psum.112
  261.0 30.6 %all-gather.13.cloned.1.call-done = bf16[1024,1024]{1,0:T(8,128)(2,1)} async-done(((bf16[1024,256]{1,0:T(8,128)(2,1)}), bf16[1024,1024]{1,0:T(8,128)(2,1)}) %all-gather.13.cloned.1.call-update) | async-done | bytes 2097168 | tf_op jit(solution)/shard_map/all_gather | solution.py:130
  291.7 4.0 multiply_reduce_fusion.5
  295.7 2.4 psum.114
  298.1 4.6 multiply_reduce_fusion.6
  304.0 2.9 convolution_convert_fusion.5
  307.0 3.5 convolution_convert_fusion
  311.3 1.9 reshape.774
  313.2 2.5 copy.200
  315.7 2.2 convolution_convert_fusion.2
  318.0 17.1 %all-gather.17.cloned.1.call-done = bf16[64,64,128]{2,1,0:T(8,128)(2,1)} async-done(((bf16[16,64,128]{2,1,0:T(8,128)(2,1)}), bf16[64,64,128]{2,1,0:T(8,128)(2,1)}) %all-gather.17.cloned.1.call-update) | async-done | bytes 1048592 | tf_op jit(solution)/shard_map/all_gather | solution.py:49
  335.1 3.7 while.116
  342.0 62.0 %while.119 = (s32[]{:T(128)}, f32[16]{0:T(128)}, f32[16,64,128]{2,1,0:T(8,128)S(1)}, f32[2,128,16,64]{1,3,2,0:T(8,128)}, f32[2,128,128]{2,1,0:T(8,128)}, /*index...) while((s32[]{:T(128)}, f32[16]{0:T(128)}, ...), condition=%wide.region_26.27_spmd.clone, body=%wide.region_16.26_spmd.clone.sunk | while | flops 1263052800 | bytes 29513872 | solution.py:202
  346.4 4.8 fusion.271
  356.9 1.7 reduce_window_sum.78
  363.0 2.3 convolution_bitcast_fusion.8
  367.0 2.0 convolution_bitcast_fusion.7
  370.0 1.9 fusion.280
  377.2 4.8 fusion.271
  394.4 2.2 convolution_bitcast_fusion.8
  398.3 2.0 convolution_bitcast_fusion.7
  401.3 1.9 fusion.280
  404.1 3.3 copy.219
  407.4 2.4 reshape.775
  409.9 1.8 fusion.113
  413.5 2.1 multiply_reduce_fusion.4
  418.1 3.8 collective-permute-done.2
  422.1 2.2 convolution_convert_fusion.1
  425.9 2.5 reduce-window.16
  428.6 2.6 fusion.195
  436.0 2.5 convolution_add_fusion.6
  441.4 16.5 %reduce-scatter.7.cloned.1.call-done = bf16[256,1024]{1,0:T(8,128)(2,1)} async-done(((bf16[1024,1024]{1,0:T(8,128)(2,1)}), bf16[256,1024]{1,0:T(8,128)(2,1)}) %reduce-scatter.7.cloned.1.call-update) | async-done | bytes 524304 | tf_op jit(solution)/shard_map/reduce_scatter | solution.py:283
  458.7 25.4 %reduce-scatter.9.cloned.1.call-done = bf16[256,16]{0,1:T(8,128)(2,1)} async-done(((bf16[1024,16]{0,1:T(8,128)(2,1)}), bf16[256,16]{0,1:T(8,128)(2,1)}) %reduce-scatter.9.cloned.1.call-update) | async-done | bytes 8208 | tf_op jit(solution)/shard_map/reduce_scatter | solution.py:286
  484.1 12.0 %psum.120 = bf16[256,16]{0,1:T(8,128)(2,1)S(1)} all-reduce(bf16[256,16]{0,1:T(8,128)(2,1)} %reduce-scatter.9.cloned.1.call-done), channel_id=1, replica_groups=mesh['dp'=4,'ctx'=4,'tensor'=2] {'ctx'}, use_global_device_ids=true, to_apply=%region_41.42 | all-reduce | flops 4096 | bytes 16384 | tf_op jit(solution)/shard_map/psum | solution.py:296
  496.7 123.7 %all-reduce.21.cloned.1.call-done = f32[1024,256]{1,0:T(8,128)} async-done(((f32[1024,256]{1,0:T(8,128)}), f32[1024,256]{1,0:T(8,128)}) %all-reduce.21.cloned.1.call-update) | async-done | bytes 1048592 | tf_op jit(solution)/shard_map/psum | solution.py:325
  622.1 19.8 %all-reduce.25.cloned.1.call-done = (bf16[256,1024]{1,0:T(8,128)(2,1)}, bf16[256,1024]{1,0:T(8,128)(2,1)}) async-done(((bf16[256,1024]{1,0:T(8,128)(2,1)}, bf16[256,1024]{1,0:T(8,128)(2,1)}), (bf16[256,1024]{1,0:T(8,128)(2,1)}, bf16[256,1024]{1,0:T(8,128)(2,1)})) %all-reduce.25.cloned.1.call-update) | async-done | bytes 1048592 | tf_op jit(solution)/shard_map/psum | solution.py:235
  643.5 44.3 %all-reduce.14 = (f32[1024]{0:T(1024)}, f32[4,2304]{1,0:T(4,128)}, f32[2304]{0:T(1024)}, f32[32]{0:T(128)}, f32[32]{0:T(128)}, /*index=5*/f32[32]{0:T(128)}, f32[2048]{0:T(1024)}) all-reduce(f32[1024]{0:T(1024)S(1)} %fusion.168, ...), channel_id=1, replica_groups=mesh['dp'=4,'ctx'=4,'tensor'=2] {'dp','ctx','tensor'}, use_global_device_ids=true, to_apply=%region_34.35 | all-reduce | flops 14688 | bytes 117504 | tf_op jit(solution)/shard_map/psum | solution.py:325
  689.4 26.2 %all-reduce.23.cloned.1.call-done = (bf16[256,1024]{1,0:T(8,128)(2,1)}, bf16[256,1024]{1,0:T(8,128)(2,1)}, bf16[1024,256]{1,0:T(8,128)(2,1)}) async-done(((bf16[256,1024]{1,0:T(8,128)(2,1)}, bf16[256,1024]{1,0:T(8,128)(2,1)}, bf16[1024,256]{1,0:T(8,128)(2,1)}), (bf16[256,1024]{1,0:T(8,128)(2,1)}, bf16[256,1024]{1,0:T(8,128)(2,1)}, bf16[1024,256]{1,0:T(8,128)(2,1)})) %all-reduce.23.cloned.1.call-update) | async-done | bytes 1572880 | tf_op jit(solution)/shard_map/psum | solution.py:294
  715.7 2.2 convert_element_type.258
  (567 shorter events, 173.5 us)
Async XLA Ops:
  7.2 22.2 %copy-start.82 = (f32[4,2304]{1,0:T(4,128)S(1)}, f32[4,2304]{1,0:T(4,128)}, u32[]{:S(2)}) copy-start(f32[4,2304]{1,0:T(4,128)} %param.37) | copy-start | bytes 110596
  7.2 22.2 %slice-start = ((f32[4,2304]{1,0:T(4,128)}), f32[4,256]{1,0:T(4,128)S(1)}, s32[]{:S(2)}) async-start(f32[4,2304]{1,0:T(4,128)} %param.37), calls=%async_computation.16 | async-start | bytes 8192 | tf_op jit(solution)/shard_map/slice | solution.py:155
  7.2 22.3 %copy-start.49 = (bf16[256,256]{1,0:T(8,128)(2,1)S(1)}, bf16[256,256]{1,0:T(8,128)(2,1)}, u32[]{:S(2)}) copy-start(bf16[256,256]{1,0:T(8,128)(2,1)} %param.35) | copy-start | bytes 393220
  7.2 42.0 %all-gather.9.cloned.1.call-start = ((), (), s32[]{:S(2)}) async-start(), calls=%async_computation.4 | async-start | bytes 2621440 | tf_op jit(solution)/shard_map/all_gather | solution.py:127
  7.9 34.8 %copy-start.103 = (f32[32]{0:T(128)S(1)}, f32[32]{0:T(128)}, u32[]{:S(2)}) copy-start(f32[32]{0:T(128)} %param.40) | copy-start | bytes 388
  8.0 35.5 %slice-start.1 = ((f32[2304]{0:T(1024)}), f32[256]{0:T(256)S(1)}, s32[]{:S(2)}) async-start(f32[2304]{0:T(1024)} %param.38), calls=%async_computation.17 | async-start | bytes 2048 | tf_op jit(solution)/shard_map/slice | solution.py:162
  8.0 35.5 %copy-start.98 = (s32[1,256]{1,0:T(1,128)S(1)}, s32[1,256]{1,0:T(1,128)}, u32[]{:S(2)}) copy-start(s32[1,256]{1,0:T(1,128)} %param.30) | copy-start | bytes 3076
  8.0 36.1 %copy-start.8 = (bf16[1,256,1024]{2,1,0:T(8,128)(2,1)S(1)}, bf16[1,256,1024]{2,1,0:T(8,128)(2,1)}, u32[]{:S(2)}) copy-start(bf16[1,256,1024]{2,1,0:T(8,128)(2,1)} %param.29) | copy-start | bytes 1572868
  8.0 36.1 %copy-start.56 = (f32[1024]{0:T(1024)S(1)}, f32[1024]{0:T(1024)}, u32[]{:S(2)}) copy-start(f32[1024]{0:T(1024)} %param.32) | copy-start | bytes 12292
  8.0 210.4 %all-gather.15.cloned.1.call-start = ((), (), s32[]{:S(2)}) async-start(), calls=%async_computation.12 | async-start | bytes 1310720 | tf_op jit(solution)/shard_map/all_gather | solution.py:24
  8.8 36.3 %copy-start.96 = (s32[256]{0:T(256)}, s32[256]{0:T(256)S(1)}, u32[]{:S(2)}) copy-start(s32[256]{0:T(256)S(1)} %get-tuple-element.2175) | copy-start | bytes 3076
  8.9 35.6 %collective-permute-start = (bf16[3]{0:T(256)(128)(2,1)S(1)}, bf16[3]{0:T(256)(128)(2,1)S(1)}, u32[]{:S(2)}, u32[]{:S(2)}) collective-permute-start(bf16[3]{0:T(256)(128)(2,1)S(1)} %slice.175), channel_id=1, source_target_pairs={{0,2},{2,4},{4,6},{1,3},{3,5},{5,7},{8,10},{10,12},{12,14},{9,11},... | collective-permute-start | bytes 26 | tf_op jit(solution)/shard_map/ppermute | solution.py:18
  24.1 5.3 copy-start.50
  24.8 19.6 %copy-start.99 = (f32[16]{0:T(128)}, f32[16]{0:T(128)S(1)}, u32[]{:S(2)}) copy-start(f32[16]{0:T(128)S(1)} %fusion.172) | copy-start | bytes 196
  26.1 16.7 %copy-start.90 = (f32[256]{0:T(256)}, f32[256]{0:T(256)S(1)}, u32[]{:S(2)}) copy-start(f32[256]{0:T(256)S(1)} %fusion.118) | copy-start | bytes 3076
  26.1 23.1 %copy-start.73 = (f32[256]{0:T(256)}, f32[256]{0:T(256)S(1)}, u32[]{:S(2)}) copy-start(f32[256]{0:T(256)S(1)} %fusion.171) | copy-start | bytes 3076
  29.5 27.0 %copy-start.59 = (f32[1280]{0:T(1024)}, f32[1280]{0:T(1024)S(1)}, u32[]{:S(2)}) copy-start(f32[1280]{0:T(1024)S(1)} %get-tuple-element.1988) | copy-start | bytes 15364
  29.5 27.0 %copy-start.61 = (f32[1280]{0:T(1024)}, f32[1280]{0:T(1024)S(1)}, u32[]{:S(2)}) copy-start(f32[1280]{0:T(1024)S(1)} %get-tuple-element.1989) | copy-start | bytes 15364
  29.5 27.0 %copy-start.63 = (f32[1280]{0:T(1024)}, f32[1280]{0:T(1024)S(1)}, u32[]{:S(2)}) copy-start(f32[1280]{0:T(1024)S(1)} %get-tuple-element.1990) | copy-start | bytes 15364
  29.5 27.0 %copy-start.65 = (f32[1280]{0:T(1024)}, f32[1280]{0:T(1024)S(1)}, u32[]{:S(2)}) copy-start(f32[1280]{0:T(1024)S(1)} %get-tuple-element.1991) | copy-start | bytes 15364
  46.3 10.2 %copy-start.84 = (f32[256]{0:T(256)}, f32[256]{0:T(256)S(1)}, u32[]{:S(2)}) copy-start(f32[256]{0:T(256)S(1)} %get-tuple-element.2214) | copy-start | bytes 3076
  46.3 10.2 %copy-start.86 = (f32[256]{0:T(256)}, f32[256]{0:T(256)S(1)}, u32[]{:S(2)}) copy-start(f32[256]{0:T(256)S(1)} %get-tuple-element.2215) | copy-start | bytes 3076
  46.3 10.2 %copy-start.88 = (f32[256]{0:T(256)}, f32[256]{0:T(256)S(1)}, u32[]{:S(2)}) copy-start(f32[256]{0:T(256)S(1)} %get-tuple-element.2216) | copy-start | bytes 3076
  51.6 4.8 collective-permute-start.1
  188.5 23.0 %copy-start.6 = (f32[2,16,64,128]{3,2,1,0:T(8,128)}, f32[2,16,64,128]{3,2,1,0:T(8,128)S(1)}, u32[]{:S(2)}) copy-start(f32[2,16,64,128]{3,2,1,0:T(8,128)S(1)} %get-tuple-element.2912) | copy-start | bytes 3145732
  188.6 4.9 copy-start.102
  188.6 6.2 copy-start.105
  188.6 19.8 %copy-start.92 = (f32[256]{0:T(256)S(1)}, f32[256]{0:T(256)}, u32[]{:S(2)}) copy-start(f32[256]{0:T(256)} %get-tuple-element.2217) | copy-start | bytes 3076
  189.4 65.5 %all-gather.11.cloned.1.call-start = ((), (), s32[]{:S(2)}) async-start(), calls=%async_computation.5 | async-start | bytes 2621440 | tf_op jit(solution)/shard_map/all_gather | solution.py:126
  190.1 101.6 %all-gather.13.cloned.1.call-start = ((), (), s32[]{:S(2)}) async-start(), calls=%async_computation.6 | async-start | bytes 2621440 | tf_op jit(solution)/shard_map/all_gather | solution.py:130
  190.7 144.4 %all-gather.17.cloned.1.call-start = ((), (), s32[]{:S(2)}) async-start(), calls=%async_computation.13 | async-start | bytes 1310720 | tf_op jit(solution)/shard_map/all_gather | solution.py:49
  192.0 26.5 %copy-start.44 = (f32[16,2,128]{2,0,1:T(8,128)}, f32[16,2,128]{2,0,1:T(8,128)S(1)}, u32[]{:S(2)}) copy-start(f32[16,2,128]{2,0,1:T(8,128)S(1)} %reduce-window.14) | copy-start | bytes 49156
  192.2 26.3 %copy-start.94 = (f32[16,2]{0,1:T(2,128)}, f32[16,2]{0,1:T(2,128)S(1)}, u32[]{:S(2)}) copy-start(f32[16,2]{0,1:T(2,128)S(1)} %slice.198) | copy-start | bytes 388
  193.5 113.5 %copy-start.47 = (f32[1024]{0:T(1024)}, f32[1024]{0:T(1024)S(1)}, u32[]{:S(2)}) copy-start(f32[1024]{0:T(1024)S(1)} %dynamic_slice.377) | copy-start | bytes 12292
  208.5 95.5 %copy-start.42 = (f32[256,16]{0,1:T(8,128)}, f32[256,16]{0,1:T(8,128)S(1)}, u32[]{:S(2)}) copy-start(f32[256,16]{0,1:T(8,128)S(1)} %fusion.149) | copy-start | bytes 49156
  218.4 4.6 copy-start.18
  226.8 28.1 %copy-start.57 = (f32[1024]{0:T(1024)S(1)}, f32[1024]{0:T(1024)}, u32[]{:S(2)}) copy-start(f32[1024]{0:T(1024)} %param.32) | copy-start | bytes 12292
  226.9 28.1 %copy-start.74 = (f32[256]{0:T(256)S(1)}, f32[256]{0:T(256)}, u32[]{:S(2)}) copy-start(f32[256]{0:T(256)} %copy-done.73) | copy-start | bytes 3076
  229.5 62.2 %copy-start.23 = (bf16[1,256,1024]{2,1,0:T(8,128)(2,1)S(1)}, bf16[1,256,1024]{2,1,0:T(8,128)(2,1)}, u32[]{:S(2)}) copy-start(bf16[1,256,1024]{2,1,0:T(8,128)(2,1)} %param.31) | copy-start | bytes 1572868
  258.6 37.1 %copy-start.13 = (f32[256,1024]{1,0:T(8,128)}, f32[256,1024]{1,0:T(8,128)S(1)}, u32[]{:S(2)}) copy-start(f32[256,1024]{1,0:T(8,128)S(1)} %get-tuple-element.2171) | copy-start | bytes 3145732
  261.0 46.0 %copy-start.70 = (f32[256]{0:T(256)}, f32[256]{0:T(256)S(1)}, u32[]{:S(2)}) copy-start(f32[256]{0:T(256)S(1)} %add_rsqrt_fusion) | copy-start | bytes 3076
  302.7 8.6 %copy-start.10 = (f32[256,1024]{1,0:T(8,128)}, f32[256,1024]{1,0:T(8,128)S(1)}, u32[]{:S(2)}) copy-start(f32[256,1024]{1,0:T(8,128)S(1)} %get-tuple-element.2164) | copy-start | bytes 3145732
  306.9 134.5 %reduce-scatter.11.cloned.1.call-start = ((), (), s32[]{:S(2)}) async-start(), calls=%async_computation.11 | async-start | bytes 2621440 | tf_op jit(solution)/shard_map/reduce_scatter | solution.py:289
  310.5 130.9 %reduce-scatter.5.cloned.1.call-start = ((), (), s32[]{:S(2)}) async-start(), calls=%async_computation.7 | async-start | bytes 2621440 | tf_op jit(solution)/shard_map/reduce_scatter | solution.py:280
  317.9 140.0 %reduce-scatter.7.cloned.1.call-start = ((), (), s32[]{:S(2)}) async-start(), calls=%async_computation.8 | async-start | bytes 2621440 | tf_op jit(solution)/shard_map/reduce_scatter | solution.py:283
  346.4 4.8 copy-start.7
  361.8 7.3 copy-start.33
  363.0 7.0 copy-start.55
  363.0 7.0 copy-start.15
  377.2 4.8 copy-start.7
  392.5 7.8 %copy-start.33 = (f32[2,128,128]{2,1,0:T(8,128)S(1)}, f32[2,128,128]{2,1,0:T(8,128)}, u32[]{:S(2)}) copy-start(f32[2,128,128]{2,1,0:T(8,128)} %get-tuple-element.2945) | copy-start | bytes 393220 | tf_op jit(solution)/shard_map/transpose(jvp())/while
  394.4 6.9 copy-start.55
  394.4 6.9 copy-start.15
  416.1 5.7 collective-permute-start.2
  424.3 4.2 copy-start.26
  424.3 59.8 %reduce-scatter.9.cloned.1.call-start = ((), (), s32[]{:S(2)}) async-start(), calls=%async_computation.10 | async-start | bytes 40960 | tf_op jit(solution)/shard_map/reduce_scatter | solution.py:286
  434.5 186.0 %all-reduce.21.cloned.1.call-start = ((), (), s32[]{:S(2)}) async-start(), calls=%async_computation.9 | async-start | bytes 2097152 | tf_op jit(solution)/shard_map/psum | solution.py:325
  436.0 205.9 %all-reduce.25.cloned.1.call-start = ((), (), s32[]{:S(2)}) async-start(), calls=%async_computation.15 | async-start | bytes 2097152 | tf_op jit(solution)/shard_map/psum | solution.py:235
  440.4 18.1 %copy-start.79 = (f32[16]{0:T(128)S(1)}, f32[16]{0:T(128)}, u32[]{:S(2)}) copy-start(f32[16]{0:T(128)} %get-tuple-element.3090) | copy-start | bytes 196
  440.5 275.2 %all-reduce.23.cloned.1.call-start = ((), (), s32[]{:S(2)}) async-start(), calls=%async_computation.14 | async-start | bytes 3145728 | tf_op jit(solution)/shard_map/psum | solution.py:294
  457.9 229.9 %copy-start.91 = (f32[256]{0:T(256)S(1)}, f32[256]{0:T(256)}, u32[]{:S(2)}) copy-start(f32[256]{0:T(256)} %copy-done.90) | copy-start | bytes 3076
  457.9 229.9 %copy-start.24 = (bf16[1,256,1024]{2,1,0:T(8,128)(2,1)S(1)}, bf16[1,256,1024]{2,1,0:T(8,128)(2,1)}, u32[]{:S(2)}) copy-start(bf16[1,256,1024]{2,1,0:T(8,128)(2,1)} %param.31) | copy-start | bytes 1572868
  641.9 46.0 %copy-start.29 = (bf16[256,1024]{1,0:T(8,128)(2,1)S(1)}, bf16[256,1024]{1,0:T(8,128)(2,1)}, u32[]{:S(2)}) copy-start(bf16[256,1024]{1,0:T(8,128)(2,1)} %get-tuple-element.2155) | copy-start | bytes 1572868
  641.9 46.0 %copy-start.39 = (bf16[256,1024]{1,0:T(8,128)(2,1)S(1)}, bf16[256,1024]{1,0:T(8,128)(2,1)}, u32[]{:S(2)}) copy-start(bf16[256,1024]{1,0:T(8,128)(2,1)} %get-tuple-element.2154) | copy-start | bytes 1572868
  (84 other events, 166.7 us)
Sparse Core Ops, SparseCore 0:
  9.9 39.2 all-gather.8
  189.5 28.9 all-gather.14
  220.3 34.5 all-gather.10
  256.6 35.0 all-gather.12
  307.1 27.9 all-gather.16
  337.9 34.5 reduce-scatter.10
  375.5 35.1 reduce-scatter.4
  424.4 33.4 reduce-scatter.6
  461.2 22.8 reduce-scatter.8
  489.7 130.6 all-reduce.20
  623.4 18.4 all-reduce.24
  644.3 71.3 all-reduce.22
where the time goes:
time: 741 us; the launch traced here: 727 us
  waiting for transfers between devices  301 us (41%)
  local copies, waits for them, and re-layouts  132 us (18%)
  blocking collectives  96.2 us (13%)
  other arithmetic  85.2 us (11%)
  matrix products  82.3 us (11%)
  between operations  18 us (2%)
  starting transfers between devices  10.1 us (1%)
    psum x1, waiting for transfers between devices, body(): lax.psum((gain_term, kernel_term, offset_term, bias_term, decay_term, ski...  124 us
    dynamic_update_slice x32, local copies, waits for them, and re-layouts, block(): lax.scan(partial(group_step, rates=rates), jnp.zeros((local_heads, head_s...  60.8 us
    psum x1, blocking collectives, body(): lax.psum((gain_term, kernel_term, offset_term, bias_term, decay_term, ski...  44.3 us
    all_gather x1, waiting for transfers between devices, body(): lax.all_gather(out_weight, 'dp', axis=1, tiled=True)  30.6 us
    psum x1, waiting for transfers between devices, body(): lax.psum(pieces[0].astype(jnp.bfloat16), 'ctx').astype(jnp.float32)  26.2 us
    reduce_scatter x1, waiting for transfers between devices, body(): lax.psum_scatter(grad_step_w.astype(jnp.bfloat16), 'dp', scatter_dimensio...  25.4 us
    all_gather x1, waiting for transfers between devices, body(): lax.all_gather(gate_weight, 'dp', axis=0, tiled=True)  25.4 us
    psum x1, waiting for transfers between devices, body(): lax.psum(branch_out.astype(jnp.bfloat16), 'tensor').astype(jnp.float32)  19.8 us
  transfers between devices with their start and end apart: 15, of which 12 were waited for; matrix products, arithmetic and copies ran while one was open for 20% of the time, Pallas kernels for 0%

commit v1 on v0

v1 whole, which is shorter than its diff:
```python
from functools import partial

import jax
import jax.numpy as jnp
from jax import lax
from jax.experimental import pallas as pl
from jax.experimental.pallas import tpu as pltpu
from jax.sharding import PartitionSpec as P

epsilon = 1e-05
highest = lax.Precision.HIGHEST
f32, bf16 = jnp.float32, jnp.bfloat16
MESH = pl.DeviceIdType.MESH
VM = pl.BlockSpec(memory_space=pltpu.VMEM)
ANY = pl.BlockSpec(memory_space=pl.ANY)
LIMIT = 56 * 1024 * 1024


def dot(a, b, ca=1, cb=0, precision=None):
    return lax.dot_general(
        a, b, (((ca,), (cb,)), ((), ())), precision=precision, preferred_element_type=f32
    )


def shifted(array, axis, by):
    size = lax.axis_size(axis)
    pairs = [(i, i + by) for i in range(size) if 0 <= i + by < size]
    return lax.ppermute(array, axis, pairs)


def chain_kernel(axis, by, chunks, local_ref, fade_ref, out_ref, landed, outgoing, send, recv):
    size = lax.axis_size(axis)
    me = lax.axis_index(axis)
    follower = lax.rem(me + by + size, size)
    leader = lax.rem(me - by + size, size)
    first, last = (0, size - 1) if by > 0 else (size - 1, 0)
    rows = local_ref.shape[0] // chunks
    barrier = pltpu.get_barrier_semaphore()

    @pl.when(me != first)
    def _():
        pl.semaphore_signal(barrier, inc=1, device_id={axis: leader}, device_id_type=MESH)

    @pl.when(me != last)
    def _():
        pl.semaphore_wait(barrier, 1)

    def copy(c):
        part = pl.ds(c * rows, rows)
        return pltpu.make_async_remote_copy(
            src_ref=outgoing.at[part],
            dst_ref=landed.at[part],
            send_sem=send.at[c],
            recv_sem=recv.at[c],
            device_id={axis: follower},
            device_id_type=MESH,
        )

    @pl.when(me == first)
    def _():
        landed[...] = jnp.zeros_like(landed)

    for c in range(chunks):
        part = pl.ds(c * rows, rows)

        @pl.when(me != first)
        def _():
            copy(c).wait_recv()

        @pl.when(me != last)
        def _():
            total = fade_ref[part, :] * landed[part, :].astype(f32) + local_ref[part, :].astype(f32)
            outgoing[part, :] = total.astype(outgoing.dtype)
            copy(c).start()

    out_ref[...] = landed[...]

    @pl.when(me != last)
    def _():
        for c in range(chunks):
            copy(c).wait_send()


def chain(local, fade, axis, by, ident, chunks=4):
    return pl.pallas_call(
        partial(chain_kernel, axis, by, chunks),
        out_shape=jax.ShapeDtypeStruct(local.shape, local.dtype),
        in_specs=[VM, VM],
        out_specs=VM,
        scratch_shapes=[
            pltpu.VMEM(local.shape, local.dtype),
            pltpu.VMEM(local.shape, local.dtype),
            pltpu.SemaphoreType.DMA((chunks,)),
            pltpu.SemaphoreType.DMA((chunks,)),
        ],
        compiler_params=pltpu.CompilerParams(collective_id=ident, has_side_effects=True),
        name="chain",
    )(local, fade)


def pair_kernel(axis, src_ref, out_ref, slots, send, recv):
    size = lax.axis_size(axis)
    me = lax.axis_index(axis)
    barrier = pltpu.get_barrier_semaphore()
    for k in range(1, size):
        pl.semaphore_signal(
            barrier, inc=1, device_id={axis: lax.rem(me + k, size)}, device_id_type=MESH
        )
    pl.semaphore_wait(barrier, size - 1)
    copies = []
    for k in range(1, size):
        copies.append(
            pltpu.make_async_remote_copy(
                src_ref=src_ref,
                dst_ref=slots.at[k - 1],
                send_sem=send.at[k - 1],
                recv_sem=recv.at[k - 1],
                device_id={axis: lax.rem(me + k, size)},
                device_id_type=MESH,
            )
        )
        copies[-1].start()
    for copy in copies:
        copy.wait()
    total = src_ref[...].astype(f32)
    for k in range(1, size):
        total = total + slots[k - 1].astype(f32)
    out_ref[...] = total


def pair_sum(array, axis, ident):
    size = lax.axis_size(axis)
    return pl.pallas_call(
        partial(pair_kernel, axis),
        out_shape=jax.ShapeDtypeStruct(array.shape, f32),
        in_specs=[VM],
        out_specs=VM,
        scratch_shapes=[
            pltpu.VMEM((size - 1,) + array.shape, array.dtype),
            pltpu.SemaphoreType.DMA((size - 1,)),
            pltpu.SemaphoreType.DMA((size - 1,)),
        ],
        compiler_params=pltpu.CompilerParams(
            collective_id=ident, has_side_effects=True, vmem_limit_bytes=LIMIT
        ),
        name="pair_sum",
    )(array)


def gather_kernel(axis, count, *refs):
    ins, outs = refs[:count], refs[count : 2 * count]
    local, send, recv = refs[2 * count :]
    me = lax.axis_index(axis)
    low, high = lax.rem(me, 2), me // 2
    side = high * 2 + (1 - low)
    other = (1 - high) * 2 + low
    corner = (1 - high) * 2 + (1 - low)
    barrier = pltpu.get_barrier_semaphore()
    for peer in (side, other):
        pl.semaphore_signal(barrier, inc=1, device_id={axis: peer}, device_id_type=MESH)
    own = []
    for a in range(count):
        own.append(pltpu.make_async_copy(ins[a], outs[a].at[me], local.at[a]))
        own[-1].start()
    pl.semaphore_wait(barrier, 2)

    def remote(a, src, dst, slot, peer):
        return pltpu.make_async_remote_copy(
            src_ref=src,
            dst_ref=dst,
            send_sem=send.at[a, slot],
            recv_sem=recv.at[a, slot],
            device_id={axis: peer},
            device_id_type=MESH,
        )

    direct = []
    for a in range(count):
        for slot, peer in ((0, side), (1, other)):
            direct.append(remote(a, ins[a], outs[a].at[me], slot, peer))
            direct[-1].start()
    relays = []
    for a in range(count):
        half = ins[a].shape[0] // 2
        lower, upper = pl.ds(0, half), pl.ds(half, half)
        remote(a, ins[a], outs[a].at[side], 0, side).wait_recv()
        relay = remote(a, outs[a].at[side, lower], outs[a].at[side, lower], 2, other)
        relay.start()
        relays.append(relay)
        remote(a, ins[a], outs[a].at[other], 1, other).wait_recv()
        relay = remote(a, outs[a].at[other, upper], outs[a].at[other, upper], 3, side)
        relay.start()
        relays.append(relay)
    for a in range(count):
        half = ins[a].shape[0] // 2
        lower, upper = pl.ds(0, half), pl.ds(half, half)
        remote(a, outs[a].at[corner, lower], outs[a].at[corner, lower], 2, other).wait_recv()
        remote(a, outs[a].at[corner, upper], outs[a].at[corner, upper], 3, side).wait_recv()
    for copy in direct + relays:
        copy.wait_send()
    for copy in own:
        copy.wait()


def gather(arrays, axis, ident):
    size = lax.axis_size(axis)
    if size != 4:
        return tuple(lax.all_gather(a, axis) for a in arrays)
    count = len(arrays)
    return pl.pallas_call(
        partial(gather_kernel, axis, count),
        out_shape=tuple(jax.ShapeDtypeStruct((size,) + a.shape, a.dtype) for a in arrays),
        in_specs=[VM] * count,
        out_specs=tuple([VM] * count),
        scratch_shapes=[
            pltpu.SemaphoreType.DMA((count,)),
            pltpu.SemaphoreType.DMA((count, 4)),
            pltpu.SemaphoreType.DMA((count, 4)),
        ],
        compiler_params=pltpu.CompilerParams(
            collective_id=ident, has_side_effects=True, vmem_limit_bytes=LIMIT
        ),
        name="gather",
    )(*arrays)


def sigmoid(v):
    return 1.0 / (1.0 + jnp.exp(-v))


def silu(v):
    return v / (1.0 + jnp.exp(-v))


def dsilu(v):
    s = sigmoid(v)
    return s * (1.0 + v * (1.0 - s))


def softplus(v):
    return jnp.maximum(v, 0.0) + jnp.log1p(jnp.exp(-jnp.abs(v)))


def spread_pair(first_lanes, table, pair):
    return jnp.where(first_lanes, table[:, 2 * pair : 2 * pair + 1], table[:, 2 * pair + 1 : 2 * pair + 2])


def lanes_first(length, head):
    return lax.broadcasted_iota(jnp.int32, (length, 2 * head), 1) < head


def negative_mask(segc, segr):
    length = segc.shape[0]
    row = lax.broadcasted_iota(jnp.int32, (length, length), 0)
    col = lax.broadcasted_iota(jnp.int32, (length, length), 1)
    return jnp.where((segc == segr) & (row >= col), 0.0, -1e30).astype(f32)


def tails(run, segc):
    length = segc.shape[0]
    return jnp.exp(run[length - 1 : length, :] - run) * (segc == segc[length - 1 : length]).astype(f32)


def local_kernel(
    width, head, cin, same, taps, offs, raw, bias, rate, segc, segr,
    tot, intra, xs, final, delta_out, run_out, runt_out, wide,
):
    length = segc.shape[0]
    total_width = cin.shape[1]
    states = (total_width - width) // 2
    wide[...] = cin[...].astype(f32)
    lags = taps.shape[0]
    pad = cin.shape[0] - length
    for c in range(total_width // 128):
        part = slice(c * 128, c * 128 + 128)
        acc = jnp.broadcast_to(offs[:, part], (length, 128))
        for j in range(lags):
            acc = acc + taps[j : j + 1, part] * (wide[pad - j : pad - j + length, part] * same[:, j : j + 1])
        tot[:, part] = acc
    delta = softplus(raw[...] + bias[...])
    delta_out[...] = delta
    row = lax.broadcasted_iota(jnp.int32, (length, length), 0)
    col = lax.broadcasted_iota(jnp.int32, (length, length), 1)
    below = (row >= col).astype(f32)
    decay = delta * rate[...]
    run = dot(below, decay, precision=highest)
    run_out[...] = run
    runt = run.T
    runt_out[...] = runt
    b = silu(tot[:, width : width + states]).astype(bf16)
    c = silu(tot[:, width + states :]).astype(bf16)
    scores = dot(c, b, 1, 1)
    negative = negative_mask(segc[...], segr[...])
    first = lanes_first(length, head)
    tail = tails(run, segc[...])
    for pair in range(width // (2 * head)):
        part = slice(pair * 2 * head, (pair + 1) * 2 * head)
        x = (silu(tot[:, part]) * spread_pair(first, delta, pair)).astype(bf16)
        xs[:, part] = x
        x32 = x.astype(f32)
        faded = (x32 * spread_pair(first, tail, pair)).astype(bf16)
        final[part, :] = dot(faded, b, 0, 0).astype(bf16)
        total = None
        for k in range(2):
            h = 2 * pair + k
            w = (jnp.exp(run[:, h : h + 1] - runt[h : h + 1, :] + negative) * scores).astype(bf16)
            xk = jnp.where(first if k == 0 else ~first, x32, 0.0).astype(bf16)
            term = dot(w, xk)
            total = term if total is None else total + term
        intra[:, part] = total


def entries(run, segc, before):
    return jnp.exp(run) * (segc == before).astype(f32)


def product_kernel(
    width, head, inner, ctot_ref, tot, intra, entering, run, segc, before, gate, gg, gain, skip, ysum, sums,
):
    length = segc.shape[0]
    first = lanes_first(length, head)
    c = silu(ctot_ref[...]).astype(bf16)
    entry = entries(run[...], segc[...], before[...])
    squares = jnp.zeros((length, 1), f32)
    project = jnp.zeros((length, 1), f32)
    for pair in range(width // (2 * head)):
        part = slice(pair * 2 * head, (pair + 1) * 2 * head)
        y = intra[:, part] + dot(c, entering[part, :], 1, 1) * spread_pair(first, entry, pair)
        ysum[:, part] = y
        mixed = y + spread_pair(first[:1], skip[...], pair) * silu(tot[:, part])
        product = mixed * silu(gate[:, part])
        squares = squares + jnp.sum(product * product, axis=1, keepdims=True)
        project = project + jnp.sum(gg[:, part] * gain[:, part] * product, axis=1, keepdims=True)
    lane = lax.broadcasted_iota(jnp.int32, sums.shape, 1)
    sums[...] = jnp.where(lane == 0, squares, jnp.where(lane == 1, project, 0.0))


def norm_kernel(
    width, head, inner, ctot_ref, tot, ysum, run, segc, before, gate, gg, gain, skip, sums,
    gated, low_gate, gm, grad_entering, grad_gain,
):
    length = segc.shape[0]
    first = lanes_first(length, head)
    c = silu(ctot_ref[...]).astype(bf16)
    entry = entries(run[...], segc[...], before[...])
    scale = lax.rsqrt(sums[:, 0:1] / inner + epsilon)
    project = scale * sums[:, 1:2] / inner
    for pair in range(width // (2 * head)):
        part = slice(pair * 2 * head, (pair + 1) * 2 * head)
        mixed = ysum[:, part] + spread_pair(first[:1], skip[...], pair) * silu(tot[:, part])
        z = gate[:, part]
        sg = sigmoid(z)
        act = z * sg
        unit = mixed * act * scale
        gated[:, part] = (unit * gain[:, part]).astype(bf16)
        g = gg[:, part]
        grad_gain[:, part] = jnp.sum(g * unit, axis=0, keepdims=True)
        gp = scale * (g * gain[:, part] - unit * project)
        gmix = gp * act
        low_gate[:, part] = (gp * mixed * sg * (1.0 + z * (1.0 - sg))).astype(bf16)
        gmb = gmix.astype(bf16)
        gm[:, part] = gmb
        scaled = (gmb.astype(f32) * spread_pair(first, entry, pair)).astype(bf16)
        grad_entering[part, :] = dot(scaled, c, 0, 0).astype(bf16)


def back_kernel(
    width, head, gm, xs, ysum, tot, cin, same, taps, raw, bias, rate, skip, delta_in, run_in, runt_in,
    segc, segr, before, entering, leaving,
    gpad, gtaps, goffs, graw, gheads, dtot, wide,
):
    length = segc.shape[0]
    heads = width // head
    total_width = tot.shape[1]
    states = (total_width - width) // 2
    first = lanes_first(length, head)
    run, runt, delta = run_in[...], runt_in[...], delta_in[...]
    negative = negative_mask(segc[...], segr[...])
    b = silu(tot[:, width : width + states]).astype(bf16)
    c = silu(tot[:, width + states :]).astype(bf16)
    scores = dot(c, b, 1, 1)
    tail = tails(run, segc[...])
    entry = entries(run, segc[...], before[...])
    dscores = jnp.zeros((length, length), f32)
    u = jnp.zeros((length, heads), f32)
    q = jnp.zeros((1, heads), f32)
    vdx = jnp.zeros((length, heads), f32)
    gv = jnp.zeros((1, heads), f32)
    ge = jnp.zeros((1, heads), f32)
    db = jnp.zeros((length, states), f32)
    dc = jnp.zeros((length, states), f32)
    chan = lax.broadcasted_iota(jnp.int32, (2 * head, heads), 0)
    which = lax.broadcasted_iota(jnp.int32, (2 * head, heads), 1)
    for pair in range(heads // 2):
        part = slice(pair * 2 * head, (pair + 1) * 2 * head)
        pick = (which == 2 * pair + (chan >= head).astype(jnp.int32)).astype(f32)
        x = xs[:, part]
        x32 = x.astype(f32)
        g = gm[:, part]
        g32 = g.astype(f32)
        tl = spread_pair(first, tail, pair)
        grad_f = leaving[part, :]
        late = dot(b, grad_f, 1, 1) * tl
        dx = late
        for k in range(2):
            h = 2 * pair + k
            lanes = first if k == 0 else ~first
            gk = jnp.where(lanes, g32, 0.0).astype(bf16)
            decay = jnp.exp(run[:, h : h + 1] - runt[h : h + 1, :] + negative)
            w = (decay * scores).astype(bf16)
            dscores = dscores + decay * dot(gk, x, 1, 1)
            dx = dx + dot(w, gk, 0, 0)
        raw_v = tot[:, part]
        sg = sigmoid(raw_v)
        v = raw_v * sg
        u = u + dot(g32 * ysum[:, part] - x32 * dx, pick, precision=highest)
        q = q + jnp.sum(dot(x32 * late, pick, precision=highest), axis=0, keepdims=True)
        vdx = vdx + dot(v * dx, pick, precision=highest)
        gv = gv + dot(jnp.sum(g32 * v, axis=0, keepdims=True), pick, precision=highest)
        per_row = jnp.sum(grad_f.astype(f32) * entering[part, :].astype(f32), axis=1, keepdims=True)
        ge = ge + jnp.sum(per_row * pick, axis=0, keepdims=True)
        dv = spread_pair(first, delta, pair) * dx + spread_pair(first[:1], skip[...], pair) * g32
        dtot[:, part] = dv * (sg * (1.0 + raw_v * (1.0 - sg)))
        db = db + dot((x32 * tl).astype(bf16), grad_f)
        dc = dc + dot((g32 * spread_pair(first, entry, pair)).astype(bf16), entering[part, :])
    dsb = dscores.astype(bf16)
    dc = dc + dot(dsb, b)
    db = db + dot(dsb, c, 0, 0)
    dtot[:, width : width + states] = db * dsilu(tot[:, width : width + states])
    dtot[:, width + states :] = dc * dsilu(tot[:, width + states :])
    row = lax.broadcasted_iota(jnp.int32, (length, length), 0)
    col = lax.broadcasted_iota(jnp.int32, (length, length), 1)
    above = (row <= col).astype(f32)
    last = slice(length - 1, length)
    dld = dot(above, u, precision=highest) + (q + entry[last, :] * ge)
    ddelta = dld * rate[...] + vdx
    gr = ddelta * sigmoid(raw[...] + bias[...])
    graw[...] = gr
    gheads[...] = jnp.zeros_like(gheads)
    gheads[0:1, :] = jnp.sum(gr, axis=0, keepdims=True)
    gheads[1:2, :] = jnp.sum(dld * delta, axis=0, keepdims=True) * rate[...]
    gheads[2:3, :] = gv
    wide[...] = cin[...].astype(f32)
    gpad[...] = jnp.zeros_like(gpad)
    lags = taps.shape[0]
    pad = cin.shape[0] - length
    for n in range(total_width // 128):
        part = slice(n * 128, n * 128 + 128)
        d = dtot[:, part]
        goffs[:, part] = jnp.sum(d, axis=0, keepdims=True)
        for j in range(lags):
            ds = d * same[:, j : j + 1]
            window = slice(pad - j, pad - j + length)
            gtaps[j : j + 1, part] = jnp.sum(ds * wide[window, part], axis=0, keepdims=True)
            gpad[window, part] = gpad[window, part] + ds * taps[j : j + 1, part]


def call(kernel, outs, args, scratch=(), name=None):
    return pl.pallas_call(
        kernel,
        out_shape=tuple(jax.ShapeDtypeStruct(s, d) for s, d in outs),
        in_specs=[VM] * len(args),
        out_specs=tuple([VM] * len(outs)),
        scratch_shapes=list(scratch),
        compiler_params=pltpu.CompilerParams(vmem_limit_bytes=LIMIT),
        name=name,
    )(*args)


def body(
    hidden,
    segment_ids,
    cotangent,
    input_gain,
    gate_weight,
    value_weight,
    state_weight,
    step_weight,
    conv_weight,
    conv_bias,
    step_bias,
    decay_log,
    skip_gain,
    mixer_gain,
    out_weight,
):
    tokens = hidden[0]
    wrapped = segment_ids[0] % 128
    cot = cotangent[0]
    length, width_in = tokens.shape
    shard = lax.axis_index("tensor")
    shards = lax.axis_size("tensor")
    lags = conv_weight.shape[0]
    reach = lags - 1
    dp = lax.axis_size("dp")
    width = gate_weight.shape[1]
    local_heads = step_weight.shape[1]
    head = width // local_heads
    inner = width * shards
    states = state_weight.shape[1] // 2
    ids_col = jnp.broadcast_to(wrapped[length - reach :].astype(bf16)[:, None], (reach, 128))
    edge = shifted(jnp.concatenate([tokens[length - reach :], ids_col], 1), "ctx", 1)
    narrow = jnp.concatenate(
        [state_weight, step_weight, jnp.zeros((state_weight.shape[0], 128 - local_heads), bf16)], 1
    )
    g_gate, g_value, g_narrow, g_out = gather(
        (gate_weight, value_weight, narrow, out_weight), "dp", 0
    )
    full_gate = g_gate.reshape(width_in, width)
    full_value = g_value.reshape(width_in, width)
    full_narrow = g_narrow.reshape(width_in, narrow.shape[1])
    full_out = jnp.concatenate([g_out[k] for k in range(dp)], 1)
    pad = 8
    base_ext = jnp.concatenate(
        [jnp.zeros((pad - reach, width_in), bf16), edge[:, :width_in], tokens], 0
    ).astype(f32)
    inv_ext = lax.rsqrt(jnp.mean(base_ext * base_ext, axis=-1, keepdims=True) + epsilon)
    normed_ext = (base_ext * inv_ext * input_gain).astype(bf16)
    normed = normed_ext[pad:]
    base = tokens.astype(f32)
    inv = inv_ext[pad:]
    gate = jnp.dot(normed, full_gate, preferred_element_type=f32)
    value_pre = jnp.dot(normed_ext, full_value, preferred_element_type=f32)
    rest_pre = jnp.dot(normed_ext, full_narrow, preferred_element_type=f32)
    cin = jnp.concatenate([value_pre.astype(bf16), rest_pre[:, : 2 * states].astype(bf16)], 1)
    raw_step = rest_pre[pad:, 2 * states : 2 * states + local_heads]
    grad_gated = jnp.dot(cot, full_out.T, preferred_element_type=f32)

    padded_ids = jnp.concatenate([edge[:, width_in].astype(jnp.int32), wrapped])
    before = padded_ids[reach - 1].astype(f32).reshape(1, 1)
    same = jnp.stack(
        [
            (padded_ids[reach - j : reach - j + length] == wrapped).astype(f32)
            for j in range(lags)
        ],
        1,
    )
    segc = wrapped.astype(f32)[:, None]
    segr = wrapped.astype(f32)[None, :]

    def local(array, size):
        return lax.dynamic_slice_in_dim(array, shard * size, size, array.ndim - 1)

    taps = jnp.concatenate([local(conv_weight, width), conv_weight[:, inner:]], 1)
    offs = jnp.concatenate([local(conv_bias, width), conv_bias[inner:]], 0)[None]
    bias = local(step_bias, local_heads)[None]
    rate = -jnp.exp(local(decay_log, local_heads))[None]
    skip = local(skip_gain, local_heads)[None]
    gain = local(mixer_gain, width)[None]
    total_width = width + 2 * states

    tot, intra, xs, final, delta, run, runt = call(
        partial(local_kernel, width, head),
        (
            ((length, total_width), f32),
            ((length, width), f32),
            ((length, width), bf16),
            ((width, states), bf16),
            ((length, local_heads), f32),
            ((length, local_heads), f32),
            ((local_heads, length), f32),
        ),
        (cin, same, taps, offs, raw_step, bias, rate, segc, segr),
        (pltpu.VMEM((length + pad, total_width), f32),),
        "mixer_local",
    )
    through = jnp.exp(run[length - 1]) * (segc[length - 1] == before[0]).astype(f32)
    fade = jnp.broadcast_to(jnp.repeat(through, head)[:, None], (width, 128))
    entering = chain(final, fade, "ctx", 1, 1)
    ctot = tot[:, width + states :]
    ysum, sums = call(
        partial(product_kernel, width, head, inner),
        (((length, width), f32), ((length, 128), f32)),
        (ctot, tot, intra, entering, run, segc, before, gate, grad_gated, gain, skip),
        (),
        "mixer_product",
    )
    sums = pair_sum(sums, "tensor", 2)
    gated, low_gate, gm, grad_entering, grad_mgain = call(
        partial(norm_kernel, width, head, inner),
        (
            ((length, width), bf16),
            ((length, width), bf16),
            ((length, width), bf16),
            ((width, states), bf16),
            ((1, width), f32),
        ),
        (ctot, tot, ysum, run, segc, before, gate, grad_gated, gain, skip, sums),
        (),
        "mixer_norm",
    )
    grad_out = jnp.dot(gated.T, cot, preferred_element_type=f32).astype(bf16)
    grad_gate_w = jnp.dot(normed.T, low_gate, preferred_element_type=f32).astype(bf16)
    out_piece = lax.psum_scatter(grad_out, "dp", scatter_dimension=1, tiled=True)
    gate_piece = lax.psum_scatter(grad_gate_w, "dp", scatter_dimension=0, tiled=True)
    leaving = chain(grad_entering, fade, "ctx", -1, 3)
    gpad, gtaps, goffs, graw, gheads = call(
        partial(back_kernel, width, head),
        (
            ((length + pad, total_width), f32),
            ((lags, total_width), f32),
            ((1, total_width), f32),
            ((length, local_heads), f32),
            ((8, local_heads), f32),
        ),
        (
            gm, xs, ysum, tot, cin, same, taps, raw_step, bias, rate, skip, delta, run, runt,
            segc, segr, before, entering, leaving,
        ),
        (pltpu.VMEM((length, total_width), f32), pltpu.VMEM((length + pad, total_width), f32)),
        "mixer_back",
    )
    edge_grad = shifted(gpad[pad - reach : pad], "ctx", -1)
    grad_input = jnp.concatenate(
        [gpad[pad : pad + length - 8], gpad[pad + length - 8 :] + jnp.pad(edge_grad, ((8 - reach, 0), (0, 0)))], 0
    )
    low_value = grad_input[:, :width].astype(bf16)
    low_rest = jnp.concatenate(
        [
            grad_input[:, width:].astype(bf16),
            graw.astype(bf16),
            jnp.zeros((length, 128 - local_heads), bf16),
        ],
        1,
    )
    low_tail = jnp.concatenate([low_value, low_rest], 1)
    grad_tail_w = jnp.dot(normed.T, low_tail, preferred_element_type=f32).astype(bf16)
    tail_piece = lax.psum_scatter(grad_tail_w, "dp", scatter_dimension=0, tiled=True)
    branch_out = jnp.dot(gated, full_out, preferred_element_type=f32).astype(bf16)
    normed_part = (
        jnp.dot(low_gate, full_gate.T, preferred_element_type=f32)
        + jnp.dot(low_value, full_value.T, preferred_element_type=f32)
        + jnp.dot(low_rest, full_narrow.T, preferred_element_type=f32)
    ).astype(bf16)
    both = pair_sum(jnp.concatenate([branch_out, normed_part], 0), "tensor", 4)
    result = (base + both[:length]).astype(bf16)
    gn = both[length:]
    grad_gain = jnp.sum(gn * base * inv, axis=0)
    gs = gn * input_gain
    grad_base = inv * (gs - base * (inv * inv) * jnp.mean(gs * base, axis=-1, keepdims=True))
    grad_tokens = cot.astype(f32) + grad_base

    out_sum = lax.psum(out_piece, "ctx").astype(f32)
    gate_sum = lax.psum(gate_piece, "ctx").astype(f32)
    tail_sum = lax.psum(tail_piece, "ctx")
    state_sum = pair_sum(tail_sum[:, width : width + 2 * states], "tensor", 5)

    mine = (shard == 0).astype(f32)

    def placed(array, size):
        spots = [jnp.where(shard == k, array, 0.0) for k in range(shards)]
        return jnp.concatenate(spots, -1)

    small = jnp.concatenate(
        [
            (grad_gain * mine)[None],
            jnp.concatenate([placed(gtaps[:, :width], width), gtaps[:, width:]], 1).reshape(1, -1),
            jnp.concatenate([placed(goffs[:, :width], width), goffs[:, width:]], 1),
            placed(grad_mgain, width),
            placed(gheads[0:1], local_heads),
            placed(gheads[1:2], local_heads),
            placed(gheads[2:3], local_heads),
        ],
        1,
    )
    sizes = [width_in, lags * (inner + 2 * states), inner + 2 * states, inner]
    sizes = sizes + [local_heads * shards] * 3
    totals = lax.psum(small, ("dp", "ctx", "tensor"))[0]
    parts, at = [], 0
    for size in sizes:
        parts.append(totals[at : at + size])
        at += size
    return (
        result[None],
        grad_tokens[None],
        parts[0],
        gate_sum,
        tail_sum[:, :width].astype(f32),
        state_sum,
        tail_sum[:, width + 2 * states : width + 2 * states + local_heads].astype(f32),
        parts[1].reshape(lags, inner + 2 * states),
        parts[2],
        parts[4],
        parts[5],
        parts[6],
        parts[3],
        out_sum,
    )


def solution(mesh):
    in_specs = (
        P("dp", "ctx", None),
        P("dp", "ctx"),
        P("dp", "ctx", None),
        P(),
        P("dp", "tensor"),
        P("dp", "tensor"),
        P("dp", None),
        P("dp", "tensor"),
        P(),
        P(),
        P(),
        P(),
        P(),
        P(),
        P("tensor", "dp"),
    )
    out_specs = (
        P("dp", "ctx", None),
        P("dp", "ctx", None),
        P(),
        P("dp", "tensor"),
        P("dp", "tensor"),
        P("dp", None),
        P("dp", "tensor"),
        P(),
        P(),
        P(),
        P(),
        P(),
        P(),
        P("tensor", "dp"),
    )
    return jax.shard_map(body, mesh=mesh, in_specs=in_specs, out_specs=out_specs, check_vma=False)
```

time: 741 us -> 367 us (0.50); the launches traced: 727 us -> 365 us
  waiting for transfers between devices: 301 us -> 89.4 us
  Pallas kernels: 0 us -> 139 us
  local copies, waits for them, and re-layouts: 132 us -> 26.6 us
  other arithmetic: 85.2 us -> 24 us
  matrix products: 82.3 us -> 22 us
  blocking collectives: 96.2 us -> 41.8 us
    psum x3 -> x1, waiting for transfers between devices: 170 us -> 21.6 us  [body(): gate_sum = lax.psum(gate_piece, 'ctx').astype(f32)]
    pallas_call x0 -> x10, Pallas kernels: none -> 139 us  [the longest x1 64.7 us: gather(): pl.pallas_call(partial(gather_kernel, axis, count), out_shape=tuple((jax....]
    all_gather x5 -> x0, waiting for transfers between devices: 82.9 us -> none  [the longest x1 30.6 us: body(): lax.all_gather(out_weight, 'dp', axis=1, tiled=True)]
    dynamic_update_slice x37 -> x0, local copies, waits for them, and re-layouts: 61.9 us -> none  [the longest x32 60.8 us: block(): lax.scan(partial(group_step, rates=rates), jnp.zeros((local_heads, head_s...]
    dot_general x42 -> x11, matrix products: 82.3 us -> 22 us  [the longest x1 3.72 us: body(): jnp.dot(normed.T, low_tail, preferred_element_type=f32).astype(bf16)]
    reduce_scatter x4 -> x3, waiting for transfers between devices: 42 us -> 65.7 us  [the longest x1 44.8 us: body(): lax.psum_scatter(grad_tail_w, 'dp', scatter_dimension=0, tiled=True)]
    all_gather x2 -> x0, blocking collectives: 21.8 us -> none  [the longest x1 13.2 us: body(): lax.all_gather(state_weight, 'dp', axis=0, tiled=True)]
    psum x4 -> x1, blocking collectives: 61.2 us -> 41.8 us  [body(): totals = lax.psum(small, ('dp', 'ctx', 'tensor'))[0]]
  transfers between devices with their start and end apart: 15 -> 6, of which waited for: 12 -> 4; matrix products, arithmetic and copies ran while one was open for 20% -> 12% of each run, Pallas kernels for 0% -> 29%
where the time goes in v1:
time: 367 us; the launch traced here: 365 us
  Pallas kernels  139 us (38%)
  waiting for transfers between devices  89.4 us (24%)
  blocking collectives  41.8 us (11%)
  local copies, waits for them, and re-layouts  26.6 us (7%)
  other arithmetic  24 us (7%)
  matrix products  22 us (6%)
  between operations  15.6 us (4%)
  starting transfers between devices  6.61 us (2%)
    pallas_call x1, Pallas kernels, gather(): pl.pallas_call(partial(gather_kernel, axis, count), out_shape=tuple((jax....  64.7 us
    reduce_scatter x1, waiting for transfers between devices, body(): lax.psum_scatter(grad_tail_w, 'dp', scatter_dimension=0, tiled=True)  44.8 us
    psum x1, blocking collectives, body(): totals = lax.psum(small, ('dp', 'ctx', 'tensor'))[0]  41.8 us
    pallas_call x2, Pallas kernels, chain(): pl.pallas_call(partial(chain_kernel, axis, by, chunks), out_shape=jax.Sha...  32.7 us
    pallas_call x4, Pallas kernels, call(): pl.pallas_call(kernel, out_shape=tuple((jax.ShapeDtypeStruct(s, d) for s,...  30.3 us
    psum x1, waiting for transfers between devices, body(): gate_sum = lax.psum(gate_piece, 'ctx').astype(f32)  21.6 us
    reduce_scatter x1, waiting for transfers between devices, body(): lax.psum_scatter(grad_out, 'dp', scatter_dimension=1, tiled=True)  20.8 us
    pallas_call x3, Pallas kernels, pair_sum(): pl.pallas_call(partial(pair_kernel, axis), out_shape=jax.ShapeDtypeStruct...  11.4 us
  transfers between devices with their start and end apart: 6, of which 4 were waited for; matrix products, arithmetic and copies ran while one was open for 12% of the time, Pallas kernels for 29%

profile of v1, /device:TPU:0, one launch (start us, length us, event | category | flops | bytes accessed | tf_op | source)
XLA Modules:
  0.0 365.1 jit_solution(1675283996416401170)
XLA Ops:
  7.2 0.7 fusion.33
  8.0 0.7 slice_bitcast_fusion.4
  8.8 4.9 %collective-permute-start = (bf16[3,1152]{1,0:T(4,128)(2,1)S(1)}, bf16[3,1152]{1,0:T(4,128)(2,1)S(1)}, u32[]{:S(2)}, u32[]{:S(2)}) collective-permute-start(bf16[3,1152]{1,0:T(4,128)(2,1)S(1)} %pad_maximum_fusion.10), channel_id=1, source_target_pairs={{0,2},{2,4},{4,6},{1,3},{3,5},{5,7},{8,10},{10,12},{12,14},{9,11},... | collective-permute-start | bytes 20744 | tf_op jit(solution)/shard_map/ppermute | solution.py:28
  13.8 0.7 constant_dynamic-slice_fusion
  14.5 0.8 dynamic_slice.19
  15.3 1.3 fusion.27.segr
  16.5 0.8 copy.41
  17.4 0.8 copy.42
  18.2 0.7 fusion.25.segc
  18.9 1.7 pad_maximum_fusion.7.refs_2_
  20.6 64.7 %gather.1 = (bf16[4,256,1024]{2,1,0:T(8,128)(2,1)}, bf16[4,256,1024]{2,1,0:T(8,128)(2,1)}, bf16[4,256,384]{2,1,0:T(8,128)(2,1)}, bf16[4,1024,256]{2,1,0:T(8,128)(2,1)}) custom-call(bf16[256,1024]{1,0:T(8,128)(2,1)} %refs_0_.1, bf16[256,1024]{1,0:T(8,128)(2,1)} %refs_1_.1, bf16[256,384]{1,0:T(8,128)(2,1)} %pad_maximum_fusion.7.refs_2_, bf16[1024,256]{1,0:T(8,128)(2,1)} %refs_3_.1), custom_call_target="tpu_custom_call" | custom-call | tf_op jit(solution)/shard_map/gather/pallas_call | solution.py:210
  85.4 2.7 slice_bitcast_fusion.3
  88.1 0.7 pad_maximum_fusion.9.taps
  89.4 3.0 convolution_bitcast_fusion.gg
  94.2 0.6 dynamic_slice.22
  96.2 0.6 slice.220.raw
  96.8 3.1 convolution_convert_fusion.3
  100.3 0.8 copy.45.same
  102.9 1.9 pad_maximum_fusion.2.cin
  104.9 7.6 %mixer_local.1 = (f32[256,1280]{1,0:T(8,128)}, f32[256,1024]{1,0:T(8,128)}, bf16[256,1024]{1,0:T(8,128)(2,1)}, bf16[1024,128]{1,0:T(8,128)(2,1)}, f32[256,16]{1,...) custom-call(bf16[264,1280]{1,0:T(8,128)(2,1)} %pad_maximum_fusion.2.cin, f32[256,4]{1,0:T(8,128)} %copy.45.same, ...), custom_call_target="tpu_custom_call" | custom-call | tf_op jit(solution)/shard_map/mixer_local/pallas_call | solution.py:459
  112.4 0.7 multiply_bitcast_fusion
  113.2 1.6 slice.176.ctot_ref
  114.8 1.7 fusion.19.gate
  116.5 1.0 broadcast_in_dim.72.fade_ref
  117.5 8.0 %chain.2.entering = bf16[1024,128]{1,0:T(8,128)(2,1)} custom-call(bf16[1024,128]{1,0:T(8,128)(2,1)} %get-tuple-element.41.local_ref, f32[1024,128]{1,0:T(8,128)} %broadcast_in_dim.72.fade_ref), custom_call_target="tpu_custom_call" | custom-call | tf_op jit(solution)/shard_map/chain/pallas_call | solution.py:85
  125.5 5.6 %mixer_product.1 = (f32[256,1024]{1,0:T(8,128)}, f32[256,128]{1,0:T(8,128)}) custom-call(f32[256,128]{1,0:T(8,128)} %slice.176.ctot_ref, f32[256,1280]{1,0:T(8,128)} %get-tuple-element.39.tot, f32[256,1024]{1,0:T(8,128)} %get-tuple-element.40.intra, bf16[1024,128]{1,0:T(8,128)(2,1)} %chain.2.entering, f32[256,16]{1,0:T(8,128)} %get-tuple-element.42.run.run_in, ...), custom_call_target="tpu_custom_call" | custom-call | tf_op jit(solution)/shard_map/mixer_product/pallas_call | solution.py:459
  131.0 2.9 pair_sum.3.sums
  134.0 5.3 %mixer_norm.1 = (bf16[256,1024]{1,0:T(8,128)(2,1)}, bf16[256,1024]{1,0:T(8,128)(2,1)}, bf16[256,1024]{1,0:T(8,128)(2,1)}, bf16[1024,128]{1,0:T(8,128)(2,1)}, f32[1,1024]{1,0:T(1,128)}) custom-call(f32[256,128]{1,0:T(8,128)} %slice.176.ctot_ref, f32[256,1280]{1,0:T(8,128)} %get-tuple-element.39.tot, f32[256,1024]{1,0:T(8,128)} %get-tuple-element.45.ysum, ...), custom_call_target="tpu_custom_call" | custom-call | tf_op jit(solution)/shard_map/mixer_norm/pallas_call | solution.py:459
  139.3 3.2 convolution_convert_fusion.2
  142.5 3.3 convolution_convert_fusion.1
  145.9 24.7 %chain.3.leaving = bf16[1024,128]{1,0:T(8,128)(2,1)} custom-call(bf16[1024,128]{1,0:T(8,128)(2,1)} %get-tuple-element.53.local_ref, f32[1024,128]{1,0:T(8,128)} %broadcast_in_dim.72.fade_ref), custom_call_target="tpu_custom_call" | custom-call | tf_op jit(solution)/shard_map/chain/pallas_call | solution.py:85
  170.7 11.8 %mixer_back.1 = (f32[264,1280]{1,0:T(8,128)}, f32[4,1280]{1,0:T(4,128)}, f32[1,1280]{1,0:T(1,128)}, f32[256,16]{1,0:T(8,128)}, f32[8,16]{1,0:T(8,128)}) custom-call(bf16[256,1024]{1,0:T(8,128)(2,1)} %get-tuple-element.49.gm, bf16[256,1024]{1,0:T(8,128)(2,1)} %get-tuple-element.50.xs, f32[256,1024]{1,0:T(8,128)} %get-tuple-element.45.ysum, ...), custom_call_target="tpu_custom_call" | custom-call | tf_op jit(solution)/shard_map/mixer_back/pallas_call | solution.py:459
  182.5 0.8 slice.187
  183.3 1.3 collective-permute-start.1
  184.6 1.4 slice.185
  185.9 0.9 convert_element_type.102
  186.8 2.1 collective-permute-done.1
  188.9 0.8 pad_add_fusion
  189.7 0.9 maximum_convert_fusion
  190.6 1.9 concatenate.56
  192.5 3.7 %convolution_convert_fusion = bf16[1024,1408]{1,0:T(8,128)(2,1)} fusion(bf16[256,1408]{1,0:T(8,128)(2,1)} %concatenate.56, bf16[264,1024]{1,0:T(8,128)(2,1)S(1)} %fusion.3), kind=kOutput, calls=%fused_computation | convolution fusion | flops 739639296 | bytes 4128768 | tf_op jit(solution)/shard_map/dot_general | solution.py:627
  197.1 0.9 broadcast_select_fusion.4
  198.1 0.7 fusion.35
  198.9 1.5 convolution_convert_fusion.4
  201.0 0.8 convolution_add_fusion.1
  201.8 20.8 %reduce-scatter.8.cloned.1.call-done = bf16[1024,256]{1,0:T(8,128)(2,1)} async-done(((bf16[1024,1024]{1,0:T(8,128)(2,1)}), bf16[1024,256]{1,0:T(8,128)(2,1)}) %reduce-scatter.8.cloned.1.call-update) | async-done | bytes 524304 | tf_op jit(solution)/shard_map/reduce_scatter | solution.py:594
  222.6 44.8 %reduce-scatter.6.cloned.1.call-done = bf16[256,1408]{1,0:T(8,128)(2,1)} async-done(((bf16[1024,1408]{1,0:T(8,128)(2,1)}), bf16[256,1408]{1,0:T(8,128)(2,1)}) %reduce-scatter.6.cloned.1.call-update) | async-done | bytes 720912 | tf_op jit(solution)/shard_map/reduce_scatter | solution.py:628
  268.5 1.0 pad_maximum_fusion.1.src_ref
  269.5 5.5 %pair_sum.4 = f32[512,1024]{1,0:T(8,128)} custom-call(bf16[512,1024]{1,0:T(8,128)(2,1)} %pad_maximum_fusion.1.src_ref), custom_call_target="tpu_custom_call" | custom-call | tf_op jit(solution)/shard_map/pair_sum/pallas_call | solution.py:133
  275.1 1.6 fusion.12
  276.8 41.8 %psum.28 = f32[1,14688]{1,0:T(1,128)S(1)} all-reduce(f32[1,14688]{1,0:T(1,128)S(1)} %concatenate.55), channel_id=1, replica_groups=mesh['dp'=4,'ctx'=4,'tensor'=2] {'dp','ctx','tensor'}, use_global_device_ids=true, to_apply=%region_3.4 | all-reduce | flops 14688 | bytes 117504 | tf_op jit(solution)/shard_map/psum | solution.py:668
  318.7 0.6 slice.233
  319.9 0.6 reshape.166
  320.6 0.6 slice_reduce_fusion.1
  321.8 3.1 fusion.9
  324.9 21.6 %all-reduce.4.cloned.1.call-done = (bf16[256,1024]{1,0:T(8,128)(2,1)}, bf16[256,1408]{1,0:T(8,128)(2,1)}, bf16[1024,256]{1,0:T(8,128)(2,1)}) async-done(((bf16[256,1024]{1,0:T(8,128)(2,1)}, bf16[256,1408]{1,0:T(8,128)(2,1)}, bf16[1024,256]{1,0:T(8,128)(2,1)}), (bf16[256,1024]{1,0:T(8,128)(2,1)}, bf16[256,1408]{1,0:T(8,128)(2,1)}, bf16[1024,256]{1,0:T(8,128)(2,1)})) %all-reduce.4.cloned.1.call-update) | async-done | bytes 1769488 | tf_op jit(solution)/shard_map/psum | solution.py:644
  346.5 2.2 slice_convert_fusion
  348.7 1.6 slice.226.src_ref
  350.2 0.8 slice_convert_fusion.2
  351.1 1.1 convert_element_type.108
  352.2 1.0 convert_element_type.113
  353.2 3.0 pair_sum.5
  356.2 0.7 copy.48
  356.9 1.7 copy.55
  (112 shorter events, 8.9 us)
Async XLA Ops:
  7.2 85.3 %copy-start = (f32[32]{0:T(128)S(1)}, f32[32]{0:T(128)}, u32[]{:S(2)}) copy-start(f32[32]{0:T(128)} %param.25) | copy-start | bytes 388
  7.2 194.6 %reduce-scatter.4.cloned.1.call-start = ((), (), s32[]{:S(2)}) async-start(), calls=%async_computation.3 | async-start | bytes 2621440 | tf_op jit(solution)/shard_map/reduce_scatter | solution.py:595
  8.8 86.0 %collective-permute-start = (bf16[3,1152]{1,0:T(4,128)(2,1)S(1)}, bf16[3,1152]{1,0:T(4,128)(2,1)S(1)}, u32[]{:S(2)}, u32[]{:S(2)}) collective-permute-start(bf16[3,1152]{1,0:T(4,128)(2,1)S(1)} %pad_maximum_fusion.10), channel_id=1, source_target_pairs={{0,2},{2,4},{4,6},{1,3},{3,5},{5,7},{8,10},{10,12},{12,14},{9,11},... | collective-permute-start | bytes 20744 | tf_op jit(solution)/shard_map/ppermute | solution.py:28
  85.3 2.8 slice-start.1
  85.3 3.5 slice-start.2
  85.3 3.4 copy-start.25
  85.3 3.4 copy-start.26
  85.4 4.0 %copy-start.8 = (bf16[1,256,1024]{2,1,0:T(8,128)(2,1)S(1)}, bf16[1,256,1024]{2,1,0:T(8,128)(2,1)}, u32[]{:S(2)}) copy-start(bf16[1,256,1024]{2,1,0:T(8,128)(2,1)} %param.17) | copy-start | bytes 1572868
  88.1 4.3 %copy-start.14 = (bf16[1024,256]{1,0:T(8,128)(2,1)}, bf16[1024,256]{1,0:T(8,128)(2,1)S(1)}, u32[]{:S(2)}) copy-start(bf16[1024,256]{1,0:T(8,128)(2,1)S(1)} %get-tuple-element.111) | copy-start | bytes 1572868
  88.1 4.3 %copy-start.16 = (bf16[1024,256]{1,0:T(8,128)(2,1)}, bf16[1024,256]{1,0:T(8,128)(2,1)S(1)}, u32[]{:S(2)}) copy-start(bf16[1024,256]{1,0:T(8,128)(2,1)S(1)} %get-tuple-element.112) | copy-start | bytes 1572868
  89.4 4.8 %copy-start.24 = (f32[2048]{0:T(1024)S(1)}, f32[2048]{0:T(1024)}, u32[]{:S(2)}) copy-start(f32[2048]{0:T(1024)} %param.28) | copy-start | bytes 24580
  89.4 5.5 %copy-start.1 = (bf16[1,256,1024]{2,1,0:T(8,128)(2,1)S(1)}, bf16[1,256,1024]{2,1,0:T(8,128)(2,1)}, u32[]{:S(2)}) copy-start(bf16[1,256,1024]{2,1,0:T(8,128)(2,1)} %param.15) | copy-start | bytes 1572868
  89.4 5.8 %copy-start.20 = (f32[1024]{0:T(1024)S(1)}, f32[1024]{0:T(1024)}, u32[]{:S(2)}) copy-start(f32[1024]{0:T(1024)} %param.18) | copy-start | bytes 12292
  89.4 6.3 %copy-start.4 = (bf16[4,256,384]{2,1,0:T(8,128)(2,1)S(1)}, bf16[4,256,384]{2,1,0:T(8,128)(2,1)}, u32[]{:S(2)}) copy-start(bf16[4,256,384]{2,1,0:T(8,128)(2,1)} %get-tuple-element.38) | copy-start | bytes 2359300
  99.9 14.9 %copy-start.2 = (bf16[4,256,1024]{2,1,0:T(8,128)(2,1)S(1)}, bf16[4,256,1024]{2,1,0:T(8,128)(2,1)}, u32[]{:S(2)}) copy-start(bf16[4,256,1024]{2,1,0:T(8,128)(2,1)} %get-tuple-element.43) | copy-start | bytes 6291460
  142.5 80.1 %reduce-scatter.8.cloned.1.call-start = ((), (), s32[]{:S(2)}) async-start(), calls=%async_computation.5 | async-start | bytes 2621440 | tf_op jit(solution)/shard_map/reduce_scatter | solution.py:594
  145.9 121.6 %reduce-scatter.6.cloned.1.call-start = ((), (), s32[]{:S(2)}) async-start(), calls=%async_computation.4 | async-start | bytes 3604480 | tf_op jit(solution)/shard_map/reduce_scatter | solution.py:628
  183.3 5.7 %collective-permute-start.1 = (f32[3,1280]{1,0:T(4,128)S(1)}, f32[3,1280]{1,0:T(4,128)S(1)}, u32[]{:S(2)}, u32[]{:S(2)}) collective-permute-start(f32[3,1280]{1,0:T(4,128)S(1)} %slice.187), channel_id=1, source_target_pairs={{2,0},{4,2},{6,4},{3,1},{5,3},{7,5},{10,8},{12,10},{14,12},{11,9},... | collective-permute-start | bytes 46088 | tf_op jit(solution)/shard_map/ppermute | solution.py:28
  196.2 0.7 copy-start.21
  196.2 0.8 copy-start.22
  196.3 1.8 copy-start.23
  196.3 1.9 copy-start.7
  196.3 150.2 %all-reduce.4.cloned.1.call-start = ((), (), s32[]{:S(2)}) async-start(), calls=%async_computation.6 | async-start | bytes 3538944 | tf_op jit(solution)/shard_map/psum | solution.py:644
  196.6 2.3 copy-start.12
  196.6 2.3 copy-start.15
  196.6 2.3 copy-start.17
  196.6 2.3 copy-start.18
  196.6 2.3 copy-start.19
  198.9 1.5 copy-start.3
  198.9 2.0 copy-start.6
  201.0 66.5 %slice-start = ((bf16[256,1280]{1,0:T(8,128)(2,1)}), bf16[256,256]{1,0:T(8,128)(2,1)S(1)}, s32[]{:S(2)}) async-start(bf16[256,1280]{1,0:T(8,128)(2,1)} %maximum_convert_fusion), calls=%async_computation.7 | async-start | bytes 262144 | tf_op jit(solution)/shard_map/slice | solution.py:620
  201.0 66.5 %copy-start.5 = (bf16[4,256,384]{2,1,0:T(8,128)(2,1)S(1)}, bf16[4,256,384]{2,1,0:T(8,128)(2,1)}, u32[]{:S(2)}) copy-start(bf16[4,256,384]{2,1,0:T(8,128)(2,1)} %get-tuple-element.38) | copy-start | bytes 2359300
  267.4 1.0 copy-start.13
  269.5 52.3 %copy-start.9 = (bf16[1,256,1024]{2,1,0:T(8,128)(2,1)S(1)}, bf16[1,256,1024]{2,1,0:T(8,128)(2,1)}, u32[]{:S(2)}) copy-start(bf16[1,256,1024]{2,1,0:T(8,128)(2,1)} %param.17) | copy-start | bytes 1572868
  346.5 4.6 %copy-start.11 = (bf16[256,1024]{1,0:T(8,128)(2,1)S(1)}, bf16[256,1024]{1,0:T(8,128)(2,1)}, u32[]{:S(2)}) copy-start(bf16[256,1024]{1,0:T(8,128)(2,1)} %get-tuple-element.104) | copy-start | bytes 1572868
  346.5 5.7 %copy-start.10 = (bf16[1024,256]{1,0:T(8,128)(2,1)S(1)}, bf16[1024,256]{1,0:T(8,128)(2,1)}, u32[]{:S(2)}) copy-start(bf16[1024,256]{1,0:T(8,128)(2,1)} %get-tuple-element.106) | copy-start | bytes 1572868
Sparse Core Ops, SparseCore 0:
  142.6 41.8 reduce-scatter.3
  187.4 35.1 reduce-scatter.7
  225.7 41.7 reduce-scatter.5
  269.9 76.5 all-reduce.3
